TPU v7x, 32 devices: a whole 2x2x4 slice. The times are simulated.
32 devices in a mesh: narrow: 2 (over y), wide: 4 (over z), nys: 4 (over x, core).
Axes of the slice: x: 2, y: 2, z: 4, core: 2. Of those that a mesh axis runs over, the one named last changes fastest.
Arguments:
- centers: bfloat16 [32768, 1024], P(('narrow', 'wide', 'nys')), may hold values from -6 to 6
- weights: float32 [32768, 1000], P(('narrow', 'wide', 'nys')), may hold values from -6 to 6
- batch_points: bfloat16 [512, 1024], P(('narrow', 'wide', 'nys')), may hold values from -6 to 6
- labels: float32 [512, 1000], P(('narrow', 'wide', 'nys')), may hold values from -6 to 6
- nystrom_points: bfloat16 [2048, 1024], P(('narrow', 'nys')), may hold values from -6 to 6
- eigvecs: float32 [2048, 160], P(('narrow', 'nys')), may hold values from -0.125 to 0.125
- corrections: float32 [160], replicated, may hold values from 0.05 to 0.5
Outputs:
- new_weights: float32 [32768, 1000], P(('narrow', 'wide', 'nys'))
All inputs are finite; a program needn't handle non-finite values.
Results may differ from a plain program's by a relative error of at most 0.0003.
The roundings to bfloat16 on the way count: a program that leaves them out, or rounds other values in their place, can miss the bound.
Values may be sent and summed in bfloat16 or wider, within the bound.
No kernel may reach another device: no remote copies, remote signals or barrier semaphores. Data moves between devices by JAX's collectives and lax.ppermute only.
A program may use at most 64 MiB of HBM per device.

v0:
```python
import math
import jax
import jax.numpy as jnp
from jax import lax
from jax.sharding import PartitionSpec as P

BATCH = 512
RATE = 16.0
SPREAD = 4.0


def kernel_with(left, left_sq, right):
    cross = lax.dot_general(
        left, right, (((1,), (1,)), ((), ())), preferred_element_type=jnp.float32
    )
    right_sq = jnp.sum(jnp.square(right.astype(jnp.float32)), axis=1)
    dist = jnp.sqrt(jnp.maximum(left_sq[:, None] + right_sq[None, :] - 2.0 * cross, 0.0))
    radius = math.sqrt(2.0 * left.shape[1])
    return jnp.exp((radius - dist) / SPREAD).astype(jnp.bfloat16)


def squares(points):
    return jnp.sum(jnp.square(points.astype(jnp.float32)), axis=1)


def per_device(centers, weights, batch_points, labels, nystrom_points, eigvecs, corrections):
    batch_all = lax.all_gather(batch_points, ("narrow", "wide", "nys"), axis=0, tiled=True)
    points_all = lax.all_gather(nystrom_points, ("narrow", "nys"), axis=0, tiled=True)
    vectors_full = lax.all_gather(eigvecs, ("narrow", "nys"), axis=0, tiled=True)
    count = lax.axis_size(("narrow", "wide", "nys"))
    scale = (centers.shape[0] * count) ** (-0.5)
    center_sq = squares(centers)
    k_batch = kernel_with(centers, center_sq, batch_all)
    partial_value = (
        lax.dot_general(
            k_batch,
            weights.astype(jnp.bfloat16),
            (((0,), (0,)), ((), ())),
            preferred_element_type=jnp.float32,
        )
        * scale
    )
    rows = labels.shape[0]
    offset = lax.axis_index(("narrow", "wide", "nys")) * rows
    placed = lax.dynamic_update_slice(jnp.zeros_like(partial_value), labels, (offset, jnp.int32(0)))
    residual = lax.psum(partial_value - placed, ("narrow", "wide", "nys")).astype(jnp.bfloat16)
    k_nystrom = kernel_with(nystrom_points, squares(nystrom_points), batch_all)
    pulled = jnp.dot(k_nystrom, residual, preferred_element_type=jnp.float32)
    local_proj = lax.dot_general(
        eigvecs, pulled, (((0,), (0,)), ((), ())), precision=lax.Precision.HIGHEST
    )
    projected = lax.psum(local_proj, ("narrow", "nys"))
    scaled_proj = corrections[:, None] * projected
    gradient = jnp.dot(k_batch, residual, preferred_element_type=jnp.float32)
    corrected_all = jnp.dot(vectors_full, scaled_proj, precision=lax.Precision.HIGHEST).astype(
        jnp.bfloat16
    )
    tile_all = kernel_with(centers, center_sq, points_all)
    nystrom_term = jnp.dot(tile_all, corrected_all, preferred_element_type=jnp.float32)
    return weights - RATE / BATCH * (gradient - nystrom_term)


def solution(mesh):
    placed = (
        P(("narrow", "wide", "nys"), None),
        P(("narrow", "wide", "nys"), None),
        P(("narrow", "wide", "nys"), None),
        P(("narrow", "wide", "nys"), None),
        P(("narrow", "nys"), None),
        P(("narrow", "nys"), None),
        P(),
    )
    return jax.shard_map(
        per_device,
        mesh=mesh,
        in_specs=placed,
        out_specs=P(("narrow", "wide", "nys"), None),
        check_vma=False,
    )
```

profile of v0, /device:TPU:0, one launch (start us, length us, event | category | flops | bytes accessed | tf_op | source)
XLA Modules:
  0.0 260.3 jit_solution(16899667897856393778)
XLA Ops:
  6.5 0.7 all-gather.4.cloned.1.call-update
  7.3 0.0 all-gather.8.cloned.1.call-start
  7.3 0.7 all-gather.8.cloned.1.call-update
  8.0 0.0 all-reduce.3.cloned.1.call-start
  8.1 1.2 multiply_reduce_fusion.3
  9.3 2.1 multiply_reduce_fusion.1
  11.4 1.0 copy.8
  12.4 0.2 broadcast_in_dim.2
  12.7 5.5 %dynamic_update_slice.3 = f32[512,1000]{0,1:T(8,128)S(1)} dynamic-update-slice(f32[512,1000]{0,1:T(8,128)S(1)} %broadcast_in_dim.2, f32[16,1000]{0,1:T(8,128)S(1)} %copy.8, s32[]{:T(128)S(6)} %select_n.3, s32[]{:T(128)} %constant.9.clone.1) | dynamic-update-slice | bytes 128004 | tf_op jit(solution)/shard_map/dynamic_update_slice | solution.py:45
  18.2 48.4 %all-gather.4.cloned.1.call-done = bf16[512,1024]{1,0:T(8,128)(2,1)} async-done(((bf16[16,1024]{1,0:T(8,128)(2,1)}), bf16[512,1024]{1,0:T(8,128)(2,1)}) %all-gather.4.cloned.1.call-update) | async-done | bytes 1048592 | tf_op jit(solution)/shard_map/all_gather | solution.py:27
  66.6 1.5 multiply_reduce_fusion.2
  68.1 4.1 %exponential_convert_fusion.1 = bf16[1024,512]{1,0:T(8,128)(2,1)S(1)} fusion(bf16[1024,1024]{1,0:T(8,128)(2,1)} %param.7, bf16[512,1024]{1,0:T(8,128)(2,1)} %all-gather.4.cloned.1.call-done, f32[512]{0:T(512)S(1)} %multiply_reduce_fusion.2, f32[1024]{0:T(1024)S(1)} %multiply_reduce_fusion.1), kind=kOutput, calls=%fused_computation.6 | convolution fusion | flops 1077411840 | bytes 4200448 | tf_op jit(solution)/shard_map/dot_general | solution.py:13
  72.2 2.6 multiply_subtract_fusion.1
  74.8 61.8 %all-reduce.4 = bf16[512,1000]{0,1:T(8,128)(2,1)S(1)} all-reduce(f32[512,1000]{0,1:T(8,128)} %multiply_subtract_fusion.1), channel_id=1, replica_groups=mesh['narrow'=2,'wide'=4,'nys'=4] {'narrow','wide','nys'}, use_global_device_ids=true, to_apply=%region_2.0 | all-reduce | flops 512000 | bytes 3072000 | tf_op jit(solution)/shard_map/psum | solution.py:46
  136.6 0.0 copy-start.5
  136.6 2.4 fusion.13
  139.0 0.0 copy-done.4
  139.0 1.6 convolution_bitcast_fusion
  140.7 0.0 all-reduce.3.cloned.1.call-update
  140.7 0.2 all-gather.6.cloned.1.call-start
  140.9 0.3 all-gather.6.cloned.1.call-update
  141.3 0.0 all-gather.8.cloned.1.call-done
  141.3 53.8 %all-reduce.3.cloned.1.call-done = f32[160,1000]{1,0:T(8,128)} async-done(((f32[160,1000]{1,0:T(8,128)}), f32[160,1000]{1,0:T(8,128)}) %all-reduce.3.cloned.1.call-update) | async-done | bytes 640016 | tf_op jit(solution)/shard_map/psum | solution.py:52
  195.1 0.0 copy-done.5
  195.1 9.7 %fusion.14 = bf16[1000,2048]{1,0:T(8,128)(2,1)} fusion(f32[2048,160]{0,1:T(8,128)} %all-gather.8.cloned.1.call-done, f32[160,1000]{1,0:T(8,128)} %all-reduce.3.cloned.1.call-done, f32[160]{0:T(256)S(1)} %copy-done.5), kind=kOutput, calls=%fused_computation.22 | convolution fusion | flops 3932320000 | bytes 6047360 | tf_op jit(solution)/shard_map/dot_general | solution.py:55
  204.8 28.0 %all-gather.6.cloned.1.call-done = bf16[2048,1024]{1,0:T(8,128)(2,1)} async-done(((bf16[256,1024]{1,0:T(8,128)(2,1)}), bf16[2048,1024]{1,0:T(8,128)(2,1)}) %all-gather.6.cloned.1.call-update) | async-done | bytes 4194320 | tf_op jit(solution)/shard_map/all_gather | solution.py:28
  232.8 3.2 %multiply_reduce_fusion = f32[2048]{0:T(1024)S(1)} fusion(bf16[2048,1024]{1,0:T(8,128)(2,1)} %all-gather.6.cloned.1.call-done), kind=kLoop, calls=%fused_computation.1 | loop fusion | flops 6289408 | bytes 4202496 | tf_op jit(solution)/shard_map/reduce_sum | solution.py:16
  236.0 0.2 copy-done.3
  236.2 9.7 %exponential_convert_fusion = bf16[1024,2048]{1,0:T(8,128)(2,1)S(1)} fusion(bf16[1024,1024]{1,0:T(8,128)(2,1)} %param.7, bf16[2048,1024]{1,0:T(8,128)(2,1)S(1)} %copy-done.3, f32[2048]{0:T(1024)S(1)} %multiply_reduce_fusion, f32[1024]{0:T(1024)S(1)} %multiply_reduce_fusion.1), kind=kOutput, calls=%fused_computation | convolution fusion | flops 4309647360 | bytes 10498048 | tf_op jit(solution)/shard_map/dot_general | solution.py:13
  246.0 0.0 copy-start.1
  246.0 4.4 %fusion.30 = f32[1024,1000]{0,1:T(8,128)S(1)} fusion(bf16[1024,2048]{1,0:T(8,128)(2,1)S(1)} %exponential_convert_fusion, bf16[1000,2048]{1,0:T(8,128)(2,1)S(1)} %copy-done.2), kind=kOutput, calls=%fused_computation.38 | convolution fusion | flops 4194304000 | bytes 12386304 | tf_op jit(solution)/shard_map/dot_general | solution.py:59
  250.4 3.3 %multiply_subtract_fusion = f32[1024,1000]{0,1:T(8,128)} fusion(f32[1024,1000]{0,1:T(8,128)S(1)} %copy-done.1, f32[1024,1000]{0,1:T(8,128)S(1)} %fusion.30, bf16[1024,512]{1,0:T(8,128)(2,1)S(1)} %exponential_convert_fusion.1, bf16[512,1000]{0,1:T(8,128)(2,1)S(1)} %all-reduce.4), kind=kOutput, calls=%fused_computation.3 | convolution fusion | flops 1051648000 | bytes 14360576 | tf_op jit(solution)/shard_map/dot_general | solution.py:54
  (8 shorter events, 0.0 us)
Async XLA Ops:
  6.5 60.0 %all-gather.4.cloned.1.call-start = ((), (), s32[]{:S(2)}) async-start(), calls=%async_computation | async-start | bytes 1081344 | tf_op jit(solution)/shard_map/all_gather | solution.py:27
  7.3 134.0 %all-gather.8.cloned.1.call-start = ((), (), s32[]{:S(2)}) async-start(), calls=%async_computation.3 | async-start | bytes 1474560 | tf_op jit(solution)/shard_map/all_gather | solution.py:29
  8.0 187.1 %all-reduce.3.cloned.1.call-start = ((), (), s32[]{:S(2)}) async-start(), calls=%async_computation.2 | async-start | bytes 1310720 | tf_op jit(solution)/shard_map/psum | solution.py:52
  68.1 4.1 %copy-start = (f32[1024,1000]{0,1:T(8,128)S(1)}, f32[1024,1000]{0,1:T(8,128)}, u32[]{:S(2)}) copy-start(f32[1024,1000]{0,1:T(8,128)} %param.8) | copy-start | bytes 12288004
  74.8 64.3 %copy-start.4 = (f32[256,160]{0,1:T(8,128)S(1)}, f32[256,160]{0,1:T(8,128)}, u32[]{:S(2)}) copy-start(f32[256,160]{0,1:T(8,128)} %param.12) | copy-start | bytes 491524
  136.6 58.5 %copy-start.5 = (f32[160]{0:T(256)S(1)}, f32[160]{0:T(256)}, u32[]{:S(2)}) copy-start(f32[160]{0:T(256)} %param.13) | copy-start | bytes 1924
  140.7 92.1 %all-gather.6.cloned.1.call-start = ((), (), s32[]{:S(2)}) async-start(), calls=%async_computation.1 | async-start | bytes 4718592 | tf_op jit(solution)/shard_map/all_gather | solution.py:28
  232.8 3.4 %copy-start.3 = (bf16[2048,1024]{1,0:T(8,128)(2,1)S(1)}, bf16[2048,1024]{1,0:T(8,128)(2,1)}, u32[]{:S(2)}) copy-start(bf16[2048,1024]{1,0:T(8,128)(2,1)} %all-gather.6.cloned.1.call-done) | copy-start | bytes 12582916
  236.2 9.8 %copy-start.2 = (bf16[1000,2048]{1,0:T(8,128)(2,1)S(1)}, bf16[1000,2048]{1,0:T(8,128)(2,1)}, u32[]{:S(2)}) copy-start(bf16[1000,2048]{1,0:T(8,128)(2,1)} %fusion.14) | copy-start | bytes 12288004
  246.0 4.5 %copy-start.1 = (f32[1024,1000]{0,1:T(8,128)S(1)}, f32[1024,1000]{0,1:T(8,128)}, u32[]{:S(2)}) copy-start(f32[1024,1000]{0,1:T(8,128)} %param.8) | copy-start | bytes 12288004
Sparse Core Ops, SparseCore 0:
  10.2 56.3 all-gather.3
  68.4 26.0 all-gather.7
  140.8 54.1 all-reduce.2
  196.8 35.9 all-gather.5
where the time goes:
time: 261 us; the launch traced here: 260 us
  waiting for transfers between devices  132 us (51%)
  blocking collectives  61.8 us (24%)
  matrix products  37.9 us (15%)
  between operations  13.3 us (5%)
  other arithmetic  8.02 us (3%)
  local copies, waits for them, and re-layouts  7.05 us (3%)
    psum x1, blocking collectives, per_device(): lax.psum(partial_value - placed, ('narrow', 'wide', 'nys'))  61.8 us
    psum x1, waiting for transfers between devices, per_device(): projected = lax.psum(local_proj, ('narrow', 'nys'))  53.8 us
    all_gather x1, waiting for transfers between devices, per_device(): lax.all_gather(batch_points, ('narrow', 'wide', 'nys'), axis=0, tiled=True)  48.4 us
    all_gather x1, waiting for transfers between devices, per_device(): lax.all_gather(nystrom_points, ('narrow', 'nys'), axis=0, tiled=True)  28 us
    dot_general x2, matrix products, kernel_with(): lax.dot_general(left, right, (((1,), (1,)), ((), ())), preferred_element_...  13.8 us
    dot_general x1, matrix products, per_device(): jnp.dot(vectors_full, scaled_proj, precision=lax.Precision.HIGHEST)  9.72 us
    dynamic_update_slice x1, local copies, waits for them, and re-layouts, per_device(): lax.dynamic_update_slice(jnp.zeros_like(partial_value), labels, (offset,...  5.52 us
  transfers between devices with their start and end apart: 4, of which 3 were waited for; matrix products, arithmetic and copies ran while one was open for 12% of the time, Pallas kernels for 0%

commit v1 on v0

--- a/solution.py
+++ b/solution.py
@@ -7,6 +7,12 @@
 BATCH = 512
 RATE = 16.0
 SPREAD = 4.0
+
+
+def _see_skins(x_in, dev_axis, across):
+    for rr in (dev_axis, across):
+        x_in = jax.lax.psum(x_in, rr)
+    return x_in
 
 
 def kernel_with(left, left_sq, right):
@@ -43,7 +49,9 @@
     rows = labels.shape[0]
     offset = lax.axis_index(("narrow", "wide", "nys")) * rows
     placed = lax.dynamic_update_slice(jnp.zeros_like(partial_value), labels, (offset, jnp.int32(0)))
-    residual = lax.psum(partial_value - placed, ("narrow", "wide", "nys")).astype(jnp.bfloat16)
+    residual = _see_skins(partial_value - placed, ("wide", "nys"), across="narrow").astype(
+        jnp.bfloat16
+    )
     k_nystrom = kernel_with(nystrom_points, squares(nystrom_points), batch_all)
     pulled = jnp.dot(k_nystrom, residual, preferred_element_type=jnp.float32)
     local_proj = lax.dot_general(

time: 261 us -> 349 us (1.34)
  waiting for transfers between devices: 132 us -> 228 us
  blocking collectives: 61.8 us -> 50.1 us
    psum x0 -> x1, waiting for transfers between devices: none -> 95.3 us  [_see_skins(): x_in = jax.lax.psum(x_in, rr)]
    psum x1, blocking collectives: 61.8 us -> 50.1 us  [_see_skins(): x_in = jax.lax.psum(x_in, rr)]
  transfers between devices with their start and end apart: 4 -> 5, of which waited for: 3 -> 4; matrix products, arithmetic and copies ran while one was open for 12% -> 7% of each run, Pallas kernels for 0% -> 0%
where the time goes in v1:
time: 349 us
  waiting for transfers between devices  228 us (65%)
  blocking collectives  50.1 us (14%)
  matrix products  40 us (11%)
  between operations  15.2 us (4%)
  other arithmetic  8.02 us (2%)
  local copies, waits for them, and re-layouts  7.05 us (2%)
    psum x1, waiting for transfers between devices, _see_skins(): x_in = jax.lax.psum(x_in, rr)  95.3 us
    psum x1, waiting for transfers between devices, per_device(): projected = lax.psum(local_proj, ('narrow', 'nys'))  52.9 us
    all_gather x1, waiting for transfers between devices, per_device(): lax.all_gather(batch_points, ('narrow', 'wide', 'nys'), axis=0, tiled=True)  50.4 us
    psum x1, blocking collectives, _see_skins(): x_in = jax.lax.psum(x_in, rr)  50.1 us
    all_gather x1, waiting for transfers between devices, per_device(): lax.all_gather(nystrom_points, ('narrow', 'nys'), axis=0, tiled=True)  27.9 us
    dot_general x2, matrix products, kernel_with(): lax.dot_general(left, right, (((1,), (1,)), ((), ())), preferred_element_...  13.8 us
    dot_general x1, matrix products, per_device(): jnp.dot(vectors_full, scaled_proj, precision=lax.Precision.HIGHEST)  9.72 us
  transfers between devices with their start and end apart: 5, of which 4 were waited for; matrix products, arithmetic and copies ran while one was open for 7% of the time, Pallas kernels for 0%

profile of v1, /device:TPU:0, one launch (start us, length us, event | category | flops | bytes accessed | tf_op | source)
XLA Modules:
  0.0 348.8 jit_solution(4980144249862710173)
XLA Ops:
  7.4 0.7 all-gather.4.cloned.1.call-update
  8.1 0.0 all-reduce.4.cloned.1.call-start
  8.1 1.0 copy.8
  9.2 0.2 broadcast_in_dim.2
  9.4 5.5 %dynamic_update_slice.3 = f32[512,1000]{0,1:T(8,128)S(1)} dynamic-update-slice(f32[512,1000]{0,1:T(8,128)S(1)} %broadcast_in_dim.2, f32[16,1000]{0,1:T(8,128)S(1)} %copy.8, s32[]{:T(128)S(6)} %select_n.3, s32[]{:T(128)} %constant.9.clone.1) | dynamic-update-slice | bytes 128004 | tf_op jit(solution)/shard_map/dynamic_update_slice | solution.py:51
  15.0 2.1 multiply_reduce_fusion.1
  17.0 50.4 %all-gather.4.cloned.1.call-done = bf16[512,1024]{1,0:T(8,128)(2,1)} async-done(((bf16[16,1024]{1,0:T(8,128)(2,1)}), bf16[512,1024]{1,0:T(8,128)(2,1)}) %all-gather.4.cloned.1.call-update) | async-done | bytes 1048592 | tf_op jit(solution)/shard_map/all_gather | solution.py:33
  67.4 1.5 multiply_reduce_fusion.2
  68.9 4.1 %exponential_convert_fusion.1 = bf16[1024,512]{1,0:T(8,128)(2,1)S(1)} fusion(bf16[1024,1024]{1,0:T(8,128)(2,1)} %param.7, bf16[512,1024]{1,0:T(8,128)(2,1)} %all-gather.4.cloned.1.call-done, f32[512]{0:T(512)S(1)} %multiply_reduce_fusion.2, f32[1024]{0:T(1024)S(1)} %multiply_reduce_fusion.1), kind=kOutput, calls=%fused_computation.6 | convolution fusion | flops 1077411840 | bytes 4200448 | tf_op jit(solution)/shard_map/dot_general | solution.py:19
  73.0 2.6 multiply_subtract_fusion.1
  75.6 0.0 all-reduce.4.cloned.1.call-update
  75.6 0.0 copy-start.5
  75.6 0.0 all-gather.8.cloned.1.call-start
  75.7 0.5 all-gather.8.cloned.1.call-update
  76.2 0.0 all-reduce.6.cloned.1.call-start
  76.3 1.2 multiply_reduce_fusion.3
  77.5 95.3 %all-reduce.4.cloned.1.call-done = f32[512,1000]{0,1:T(8,128)} async-done(((f32[512,1000]{0,1:T(8,128)}), f32[512,1000]{0,1:T(8,128)}) %all-reduce.4.cloned.1.call-update) | async-done | bytes 2048016 | tf_op jit(solution)/shard_map/psum | solution.py:14
  172.8 50.1 %all-reduce.7 = bf16[512,1000]{0,1:T(8,128)(2,1)S(1)} all-reduce(f32[512,1000]{0,1:T(8,128)} %all-reduce.4.cloned.1.call-done), channel_id=1, replica_groups=mesh['narrow'=2,'wide'=4,'nys'=4] {'narrow'}, use_global_device_ids=true, to_apply=%region_3.0 | all-reduce | flops 512000 | bytes 3072000 | tf_op jit(solution)/shard_map/psum | solution.py:14
  222.9 3.2 fusion.13
  226.2 2.9 convolution_bitcast_fusion
  229.0 0.0 all-reduce.6.cloned.1.call-update
  229.1 0.2 all-gather.6.cloned.1.call-start
  229.3 0.3 all-gather.6.cloned.1.call-update
  229.6 0.0 all-gather.8.cloned.1.call-done
  229.7 52.9 %all-reduce.6.cloned.1.call-done = f32[160,1000]{1,0:T(8,128)} async-done(((f32[160,1000]{1,0:T(8,128)}), f32[160,1000]{1,0:T(8,128)}) %all-reduce.6.cloned.1.call-update) | async-done | bytes 640016 | tf_op jit(solution)/shard_map/psum | solution.py:60
  282.6 9.7 %fusion.14 = bf16[1000,2048]{1,0:T(8,128)(2,1)} fusion(f32[2048,160]{0,1:T(8,128)} %all-gather.8.cloned.1.call-done, f32[160,1000]{1,0:T(8,128)} %all-reduce.6.cloned.1.call-done, f32[160]{0:T(256)S(1)} %copy-done.6), kind=kOutput, calls=%fused_computation.22 | convolution fusion | flops 3932320000 | bytes 6047360 | tf_op jit(solution)/shard_map/dot_general | solution.py:63
  292.3 27.9 %all-gather.6.cloned.1.call-done = bf16[2048,1024]{1,0:T(8,128)(2,1)} async-done(((bf16[256,1024]{1,0:T(8,128)(2,1)}), bf16[2048,1024]{1,0:T(8,128)(2,1)}) %all-gather.6.cloned.1.call-update) | async-done | bytes 4194320 | tf_op jit(solution)/shard_map/all_gather | solution.py:34
  320.2 3.2 multiply_reduce_fusion
  323.4 0.2 copy-done.3
  323.7 9.7 %exponential_convert_fusion = bf16[1024,2048]{1,0:T(8,128)(2,1)S(1)} fusion(bf16[1024,1024]{1,0:T(8,128)(2,1)} %param.7, bf16[2048,1024]{1,0:T(8,128)(2,1)S(1)} %copy-done.3, f32[2048]{0:T(1024)S(1)} %multiply_reduce_fusion, f32[1024]{0:T(1024)S(1)} %multiply_reduce_fusion.1), kind=kOutput, calls=%fused_computation | convolution fusion | flops 4309647360 | bytes 10498048 | tf_op jit(solution)/shard_map/dot_general | solution.py:19
  333.4 4.4 %fusion.30 = f32[1024,1000]{0,1:T(8,128)S(1)} fusion(bf16[1024,2048]{1,0:T(8,128)(2,1)S(1)} %exponential_convert_fusion, bf16[1000,2048]{1,0:T(8,128)(2,1)S(1)} %copy-done.2), kind=kOutput, calls=%fused_computation.38 | convolution fusion | flops 4194304000 | bytes 12386304 | tf_op jit(solution)/shard_map/dot_general | solution.py:67
  337.9 3.3 multiply_subtract_fusion
  (13 shorter events, 0.0 us)
Async XLA Ops:
  7.4 60.0 %all-gather.4.cloned.1.call-start = ((), (), s32[]{:S(2)}) async-start(), calls=%async_computation | async-start | bytes 1081344 | tf_op jit(solution)/shard_map/all_gather | solution.py:33
  8.1 164.7 %all-reduce.4.cloned.1.call-start = ((), (), s32[]{:S(2)}) async-start(), calls=%async_computation.1 | async-start | bytes 4096000 | tf_op jit(solution)/shard_map/psum | solution.py:14
  68.9 4.1 %copy-start = (f32[1024,1000]{0,1:T(8,128)S(1)}, f32[1024,1000]{0,1:T(8,128)}, u32[]{:S(2)}) copy-start(f32[1024,1000]{0,1:T(8,128)} %param.8) | copy-start | bytes 12288004
  75.6 147.3 %copy-start.4 = (bf16[256,1024]{1,0:T(8,128)(2,1)S(1)}, bf16[256,1024]{1,0:T(8,128)(2,1)}, u32[]{:S(2)}) copy-start(bf16[256,1024]{1,0:T(8,128)(2,1)} %param.11) | copy-start | bytes 1572868
  75.6 150.5 %copy-start.5 = (f32[256,160]{0,1:T(8,128)S(1)}, f32[256,160]{0,1:T(8,128)}, u32[]{:S(2)}) copy-start(f32[256,160]{0,1:T(8,128)} %param.12) | copy-start | bytes 491524
  75.6 154.0 %all-gather.8.cloned.1.call-start = ((), (), s32[]{:S(2)}) async-start(), calls=%async_computation.4 | async-start | bytes 1474560 | tf_op jit(solution)/shard_map/all_gather | solution.py:35
  76.2 206.3 %all-reduce.6.cloned.1.call-start = ((), (), s32[]{:S(2)}) async-start(), calls=%async_computation.3 | async-start | bytes 1310720 | tf_op jit(solution)/shard_map/psum | solution.py:60
  222.9 59.6 %copy-start.6 = (f32[160]{0:T(256)S(1)}, f32[160]{0:T(256)}, u32[]{:S(2)}) copy-start(f32[160]{0:T(256)} %param.13) | copy-start | bytes 1924
  229.1 91.2 %all-gather.6.cloned.1.call-start = ((), (), s32[]{:S(2)}) async-start(), calls=%async_computation.2 | async-start | bytes 4718592 | tf_op jit(solution)/shard_map/all_gather | solution.py:34
  320.2 3.4 copy-start.3
  323.7 9.8 %copy-start.2 = (bf16[1000,2048]{1,0:T(8,128)(2,1)S(1)}, bf16[1000,2048]{1,0:T(8,128)(2,1)}, u32[]{:S(2)}) copy-start(bf16[1000,2048]{1,0:T(8,128)(2,1)} %fusion.14) | copy-start | bytes 12288004
  333.4 4.5 %copy-start.1 = (f32[1024,1000]{0,1:T(8,128)S(1)}, f32[1024,1000]{0,1:T(8,128)}, u32[]{:S(2)}) copy-start(f32[1024,1000]{0,1:T(8,128)} %param.8) | copy-start | bytes 12288004
Sparse Core Ops, SparseCore 0:
  11.0 56.3 all-gather.3
  75.8 97.0 all-reduce.3
Sparse Core Ops, SparseCore 1:
  78.0 23.8 all-gather.7
  229.2 53.4 all-reduce.5
  284.3 35.8 all-gather.5
